TPU v7x, 256 devices: a whole 4x4x8 slice. The times are simulated.
256 devices in a mesh: node: 16 (over x, y), tile: 16 (over z, core).
Axes of the slice: x: 4, y: 4, z: 8, core: 2. Of those that a mesh axis runs over, the one named last changes fastest.
Arguments:
- schur: float32 [16, 1536, 24576], P(None, 'tile', 'node'), may hold values from -0.0390625 to 0.0390625
- samples: float32 [16, 1536, 512], P(None, 'tile'), may hold values from -6 to 6
Outputs:
- leaf_basis: float32 [16, 1536, 512], P('node', 'tile')
- level_one: float32 [16, 512, 512], P('node', 'tile')
- level_two: float32 [16, 512, 512], P('node', 'tile')
All inputs are finite; a program needn't handle non-finite values.
Results may differ from a plain program's by a relative error of at most 0.00011.
Values sent between devices are 32-bit elements; how exact they have to be, the bound alone decides.
A program may use at most 128 MiB of HBM per device.

v0:
```python
import math
import jax
import jax.numpy as jnp
from jax import lax
from jax.sharding import PartitionSpec as P

HIGH = lax.Precision.HIGHEST


def swap(block, axis, mask):
    count = lax.axis_size(axis)
    return lax.ppermute(block, axis, [(low, low ^ mask) for low in range(count)])


def product(left, right):
    return jnp.dot(left, right, precision=HIGH, preferred_element_type=jnp.float32)


def transposed(left, right):
    return lax.dot_general(
        left, right, (((0,), (0,)), ((), ())), precision=HIGH, preferred_element_type=jnp.float32
    )


def inverse_lower(factor):
    eye = jnp.eye(factor.shape[0], dtype=factor.dtype)
    return jax.scipy.linalg.solve_triangular(factor, eye, lower=True)


def tile_bits():
    return [bit for bit in range(lax.axis_size("tile").bit_length() - 1)]


def halve(block):
    tile = lax.axis_index("tile")
    for bit in tile_bits():
        side = tile >> bit & 1
        half = block.shape[0] // 2
        keep = lax.dynamic_slice_in_dim(block, side * half, half, 0)
        send = lax.dynamic_slice_in_dim(block, (1 - side) * half, half, 0)
        block = keep + swap(send, "tile", 1 << bit)
    return block


def double(block, dim):
    tile = lax.axis_index("tile")
    for bit in reversed(tile_bits()):
        side = tile >> bit & 1
        other = swap(block, "tile", 1 << bit)
        block = jnp.where(
            side == 0,
            jnp.concatenate([block, other], axis=dim),
            jnp.concatenate([other, block], axis=dim),
        )
    return block


def chunk_rows(block, count):
    tile = lax.axis_index("tile")
    start = 0
    size = block.shape[0]
    for bit in tile_bits():
        size //= 2
        start = start + (tile >> bit & 1) * size
    return lax.dynamic_slice_in_dim(block, start, count, 0)


def on_device(schur, samples):
    leaves, slice_cols, leaf_rows = schur.shape
    rank_size = samples.shape[2]
    node = lax.axis_index("node")
    tile = lax.axis_index("tile")
    tile_count = lax.axis_size("tile")
    out_rows = rank_size // tile_count
    owned = lax.dynamic_index_in_dim(samples, node, 0, keepdims=False)
    keep = (jnp.arange(leaves, dtype=jnp.int32) != node)[:, None, None]
    masked = jnp.where(keep, samples, 0.0).reshape(leaves * slice_cols, rank_size)
    stacked = schur.reshape(leaves * slice_cols, leaf_rows)
    sample_rows = lax.psum_scatter(
        transposed(stacked, masked), "tile", scatter_dimension=0, tiled=True
    )
    both = lax.all_gather(jnp.concatenate([sample_rows, owned], axis=1), "tile", axis=0, tiled=True)
    local = both[:, :rank_size]
    omega = both[:, rank_size:]
    factor = jnp.linalg.cholesky(transposed(local, local))
    basis = product(local, inverse_lower(factor).T)
    reduced = transposed(basis, omega)
    basis_rows = lax.dynamic_slice_in_dim(basis, tile * slice_cols, slice_cols, 0)

    def meet(target):
        piece = lax.dynamic_index_in_dim(schur, target, 0, keepdims=False)
        return product(piece, basis)

    panel_one = product(basis_rows, reduced)
    sibling_rows = swap(panel_one, "node", 1)
    other_reduced = swap(reduced, "node", 1)
    near_meet = meet(jnp.bitwise_xor(node, 1))
    cousin_meet = meet(jnp.bitwise_xor(node, 2))
    further_meet = meet(jnp.bitwise_xor(node, 3))
    near_part = halve(transposed(near_meet, sibling_rows))
    sample_part = chunk_rows(factor.T, near_part.shape[0]) - near_part
    other_part = swap(sample_part, "node", 1)
    pair = double(jnp.stack([sample_part, other_part]), 1)
    parent_sample, other_sample = (pair[0], pair[1])
    parent_factor = jnp.linalg.cholesky(
        transposed(parent_sample, parent_sample) + transposed(other_sample, other_sample)
    )
    parent_inverse = inverse_lower(parent_factor).T
    transfer_own = product(parent_sample, parent_inverse)
    transfer_other = product(other_sample, parent_inverse)
    parent_reduced = transposed(transfer_own, reduced) + transposed(transfer_other, other_reduced)
    panel_two = product(basis_rows, product(transfer_own, parent_reduced))
    cousin_rows = swap(panel_two, "node", 2)
    further_rows = swap(panel_two, "node", 3)
    far_sum = transposed(cousin_meet, cousin_rows) + transposed(further_meet, further_rows)
    far_part = halve(transposed(transfer_own, far_sum))
    far_pair = far_part + swap(far_part, "node", 1)
    grand_part = chunk_rows(parent_factor.T, far_pair.shape[0]) - far_pair
    cousin_part = swap(grand_part, "node", 2)
    grand_pair = double(jnp.stack([grand_part, cousin_part]), 1)
    grand_sample, cousin_grand = (grand_pair[0], grand_pair[1])
    grand_factor = jnp.linalg.cholesky(
        transposed(grand_sample, grand_sample) + transposed(cousin_grand, cousin_grand)
    )
    grand_transfer = product(grand_sample, inverse_lower(grand_factor).T)
    leaf_out = (basis_rows * math.sqrt(leaf_rows))[None]
    one_rows = lax.dynamic_slice_in_dim(transfer_own, tile * out_rows, out_rows, 0)
    level_one = (one_rows * math.sqrt(2 * rank_size))[None]
    two_rows = product(one_rows, grand_transfer)
    level_two = (two_rows * (2.0 * math.sqrt(rank_size)))[None]
    return (leaf_out, level_one, level_two)


def solution(mesh):
    placed = (P(None, "tile", "node"), P(None, "tile", None))
    return jax.shard_map(
        on_device,
        mesh=mesh,
        in_specs=placed,
        out_specs=(P("node", "tile", None), P("node", "tile", None), P("node", "tile", None)),
        check_vma=False,
    )
```

profile of v0, /device:TPU:1, one launch (start us, length us, event | category | flops | bytes accessed | tf_op | source)
XLA Modules:
  0.0 900.6 jit_solution(1732461360240981253)
XLA Ops:
  7.2 18.4 %convolution_bitcast_fusion = f32[1536,512]{0,1:T(8,128)S(1)} fusion(f32[16,96,1536]{2,1,0:T(8,128)} %param.5, f32[16,96,512]{2,1,0:T(8,128)} %param.6, pred[16]{0:T(512)(128)(4,1)S(1)} %iota_compare_fusion.4), kind=kOutput, calls=%fused_computation.6 | convolution fusion | flops 14496301056 | bytes 15728656 | tf_op jit(solution)/shard_map/dot_general | solution.py:20
  29.4 60.6 %reduce-scatter.4.cloned.1.call-done = f32[96,512]{1,0:T(8,128)} async-done(((f32[1536,512]{1,0:T(8,128)}), f32[96,512]{1,0:T(8,128)}) %reduce-scatter.4.cloned.1.call-update) | async-done | bytes 196624
  92.2 48.0 %all-gather.2.cloned.1.call-done = f32[1536,1024]{1,0:T(8,128)} async-done(((f32[96,1024]{1,0:T(8,128)}), f32[1536,1024]{1,0:T(8,128)}) %all-gather.2.cloned.1.call-update) | async-done | bytes 6291472 | tf_op jit(solution)/shard_map/all_gather | solution.py:82
  140.2 8.0 fusion.5
  149.7 11.7 %cholesky.374 = f32[128,128]{1,0:T(8,128)S(1)} custom-call(f32[128,128]{1,0:T(8,128)S(1)} %cholesky.586), custom_call_target="Cholesky" | custom-call | tf_op jit(solution)/shard_map/jit(cholesky)/cholesky | solution.py:85
  161.5 10.0 %custom-call.31 = f32[1,128,128]{1,2,0:T(8,128)S(1)} custom-call(f32[1,128,128]{2,1,0:T(8,128)S(1)} %get-tuple-element.91), custom_call_target="InvertDiagBlocksLowerTriangular" | custom-call | tf_op jit(solution)/shard_map/jit(cholesky)/cholesky | solution.py:85
  174.5 11.7 %cholesky.393 = f32[128,128]{1,0:T(8,128)S(1)} custom-call(f32[128,128]{1,0:T(8,128)S(1)} %cholesky.590), custom_call_target="Cholesky" | custom-call | tf_op jit(solution)/shard_map/jit(cholesky)/cholesky | solution.py:85
  186.3 9.8 %custom-call.32 = f32[1,128,128]{1,2,0:T(8,128)S(1)} custom-call(f32[1,128,128]{2,1,0:T(8,128)S(1)} %get-tuple-element.88), custom_call_target="InvertDiagBlocksLowerTriangular" | custom-call | tf_op jit(solution)/shard_map/jit(cholesky)/cholesky | solution.py:85
  197.7 11.7 %cholesky.414 = f32[128,128]{1,0:T(8,128)S(1)} custom-call(f32[128,128]{1,0:T(8,128)S(1)} %cholesky.595), custom_call_target="Cholesky" | custom-call | tf_op jit(solution)/shard_map/jit(cholesky)/cholesky | solution.py:85
  210.1 10.2 %custom-call.33 = f32[1,128,128]{1,2,0:T(8,128)S(1)} custom-call(f32[1,128,128]{2,1,0:T(8,128)S(1)} %get-tuple-element.85), custom_call_target="InvertDiagBlocksLowerTriangular" | custom-call | tf_op jit(solution)/shard_map/jit(cholesky)/cholesky | solution.py:85
  221.7 11.7 %cholesky.431 = f32[128,128]{1,0:T(8,128)S(1)} custom-call(f32[128,128]{1,0:T(8,128)S(1)} %convolution_subtract_fusion.17), custom_call_target="Cholesky" | custom-call | tf_op jit(solution)/shard_map/jit(cholesky)/cholesky | solution.py:85
  238.7 8.0 while.6
  246.7 39.5 %custom-call.34 = f32[4,128,128]{1,2,0:T(8,128)S(1)} custom-call(f32[4,128,128]{2,1,0:T(8,128)S(1)} %get-tuple-element.25), custom_call_target="InvertDiagBlocksLowerTriangular" | custom-call | tf_op jit(solution)/shard_map/jit(_solve_triangular)/triangular_solve | solution.py:27
  289.4 7.3 fusion.3
  296.7 5.4 fusion
  317.4 6.7 collective-permute-done.2
  327.8 12.6 %collective-permute-done.3 = f32[64,512]{0,1:T(8,128)} collective-permute-done((f32[64,512]{0,1:T(8,128)S(1)}, f32[64,512]{0,1:T(8,128)}, u32[]{:S(2)}, u32[]{:S(2)}) %collective-permute-start.3) | collective-permute-done | bytes 131104 | tf_op jit(solution)/shard_map/ppermute | solution.py:12
  344.9 14.9 %collective-permute-done.4 = f32[32,512]{0,1:T(8,128)} collective-permute-done((f32[32,512]{0,1:T(8,128)}, f32[32,512]{0,1:T(8,128)}, u32[]{:S(2)}, u32[]{:S(2)}) %collective-permute-start.4) | collective-permute-done | bytes 65568 | tf_op jit(solution)/shard_map/ppermute | solution.py:12
  364.0 5.3 collective-permute-done.5
  372.3 5.0 collective-permute-done.6
  378.5 14.7 %collective-permute-done.7 = f32[2,64,512]{2,1,0:T(8,128)} collective-permute-done((f32[2,64,512]{2,1,0:T(8,128)S(1)}, f32[2,64,512]{2,1,0:T(8,128)}, u32[]{:S(2)}, u32[]{:S(2)}) %collective-permute-start.7) | collective-permute-done | bytes 262176 | tf_op jit(solution)/shard_map/ppermute | solution.py:12
  395.1 13.3 %collective-permute-done.8 = f32[2,128,512]{2,1,0:T(8,128)} collective-permute-done((f32[2,128,512]{2,1,0:T(8,128)}, f32[2,128,512]{2,1,0:T(8,128)}, u32[]{:S(2)}, u32[]{:S(2)}) %collective-permute-start.8) | collective-permute-done | bytes 524320 | tf_op jit(solution)/shard_map/ppermute | solution.py:12
  430.1 11.7 %cholesky.446 = f32[128,128]{1,0:T(8,128)S(1)} custom-call(f32[128,128]{1,0:T(8,128)S(1)} %cholesky.599), custom_call_target="Cholesky" | custom-call | tf_op jit(solution)/shard_map/jit(cholesky)/cholesky | solution.py:105
  442.4 10.6 %custom-call.35 = f32[1,128,128]{1,2,0:T(8,128)} custom-call(f32[1,128,128]{2,1,0:T(8,128)S(1)} %get-tuple-element.81), custom_call_target="InvertDiagBlocksLowerTriangular" | custom-call | tf_op jit(solution)/shard_map/jit(cholesky)/cholesky | solution.py:105
  458.6 11.7 %cholesky.465 = f32[128,128]{1,0:T(8,128)S(1)} custom-call(f32[128,128]{1,0:T(8,128)S(1)} %cholesky.603), custom_call_target="Cholesky" | custom-call | tf_op jit(solution)/shard_map/jit(cholesky)/cholesky | solution.py:105
  473.9 9.8 %custom-call.36 = f32[1,128,128]{1,2,0:T(8,128)S(1)} custom-call(f32[1,128,128]{2,1,0:T(8,128)S(1)} %get-tuple-element.78), custom_call_target="InvertDiagBlocksLowerTriangular" | custom-call | tf_op jit(solution)/shard_map/jit(cholesky)/cholesky | solution.py:105
  487.0 12.3 %cholesky.486 = f32[128,128]{1,0:T(8,128)} custom-call(f32[128,128]{1,0:T(8,128)S(1)} %cholesky.608), custom_call_target="Cholesky" | custom-call | tf_op jit(solution)/shard_map/jit(cholesky)/cholesky | solution.py:105
  501.5 10.6 %custom-call.37 = f32[1,128,128]{1,2,0:T(8,128)} custom-call(f32[1,128,128]{2,1,0:T(8,128)S(1)} %get-tuple-element.75), custom_call_target="InvertDiagBlocksLowerTriangular" | custom-call | tf_op jit(solution)/shard_map/jit(cholesky)/cholesky | solution.py:105
  515.2 11.7 %cholesky.503 = f32[128,128]{1,0:T(8,128)S(1)} custom-call(f32[128,128]{1,0:T(8,128)S(1)} %convolution_subtract_fusion.16), custom_call_target="Cholesky" | custom-call | tf_op jit(solution)/shard_map/jit(cholesky)/cholesky | solution.py:105
  534.4 14.0 %while.7 = (s32[]{:T(128)}, f32[512,512]{1,0:T(8,128)}, s32[4,2]{0,1:T(2,128)S(1)}, f32[4,128,128]{2,1,0:T(8,128)}, s32[]{:T(128)}) while((s32[]{:T(128)}, f32[512,512]{1,0:T(8,128)}, s32[4,2]{0,1:T(2,128)S(1)}, f32[4,128,128]{2,1,0:T(8,128)}, s32[]{:T(128)}) %tuple.89), condition=%wide.while_cond.clone, body=%wide.while_body.clone.sunk | while | flops 2 | bytes 132705 | solution.py:27
  548.3 41.1 %custom-call.38 = f32[4,128,128]{1,2,0:T(8,128)} custom-call(f32[4,128,128]{2,1,0:T(8,128)} %get-tuple-element.26), custom_call_target="InvertDiagBlocksLowerTriangular" | custom-call | tf_op jit(solution)/shard_map/jit(_solve_triangular)/triangular_solve | solution.py:27
  628.0 7.5 collective-permute-done.14
  635.8 14.5 %collective-permute-done.15 = f32[64,512]{0,1:T(8,128)S(1)} collective-permute-done((f32[64,512]{0,1:T(8,128)S(1)}, f32[64,512]{0,1:T(8,128)S(1)}, u32[]{:S(2)}, u32[]{:S(2)}) %collective-permute-start.15) | collective-permute-done | bytes 131104 | tf_op jit(solution)/shard_map/ppermute | solution.py:12
  652.3 14.7 %collective-permute-done.16 = f32[32,512]{0,1:T(8,128)S(1)} collective-permute-done((f32[32,512]{0,1:T(8,128)S(1)}, f32[32,512]{0,1:T(8,128)S(1)}, u32[]{:S(2)}, u32[]{:S(2)}) %collective-permute-start.16) | collective-permute-done | bytes 65568 | tf_op jit(solution)/shard_map/ppermute | solution.py:12
  667.5 7.1 collective-permute-done.17
  676.5 7.3 collective-permute-done.18
  686.2 6.5 collective-permute-done.19
  693.2 13.6 %collective-permute-done.20 = f32[2,64,512]{2,1,0:T(8,128)S(1)} collective-permute-done((f32[2,64,512]{2,1,0:T(8,128)S(1)}, f32[2,64,512]{2,1,0:T(8,128)S(1)}, u32[]{:S(2)}, u32[]{:S(2)}) %collective-permute-start.20) | collective-permute-done | bytes 262176 | tf_op jit(solution)/shard_map/ppermute | solution.py:12
  707.0 12.1 %collective-permute-done.21 = f32[2,128,512]{2,1,0:T(8,128)S(1)} collective-permute-done((f32[2,128,512]{2,1,0:T(8,128)S(1)}, f32[2,128,512]{2,1,0:T(8,128)S(1)}, u32[]{:S(2)}, u32[]{:S(2)}) %collective-permute-start.21) | collective-permute-done | bytes 524320 | tf_op jit(solution)/shard_map/ppermute | solution.py:12
  735.5 11.7 %cholesky.518 = f32[128,128]{1,0:T(8,128)S(1)} custom-call(f32[128,128]{1,0:T(8,128)S(1)} %cholesky.612), custom_call_target="Cholesky" | custom-call | tf_op jit(solution)/shard_map/jit(cholesky)/cholesky | solution.py:122
  748.3 9.8 %custom-call.39 = f32[1,128,128]{1,2,0:T(8,128)S(1)} custom-call(f32[1,128,128]{2,1,0:T(8,128)S(1)} %get-tuple-element.71), custom_call_target="InvertDiagBlocksLowerTriangular" | custom-call | tf_op jit(solution)/shard_map/jit(cholesky)/cholesky | solution.py:122
  761.4 11.9 %cholesky.537 = f32[128,128]{1,0:T(8,128)S(1)} custom-call(f32[128,128]{1,0:T(8,128)S(1)} %cholesky.616), custom_call_target="Cholesky" | custom-call | tf_op jit(solution)/shard_map/jit(cholesky)/cholesky | solution.py:122
  775.3 9.8 %custom-call.40 = f32[1,128,128]{1,2,0:T(8,128)S(1)} custom-call(f32[1,128,128]{2,1,0:T(8,128)S(1)} %get-tuple-element.68), custom_call_target="InvertDiagBlocksLowerTriangular" | custom-call | tf_op jit(solution)/shard_map/jit(cholesky)/cholesky | solution.py:122
  787.5 11.7 %cholesky.558 = f32[128,128]{1,0:T(8,128)S(1)} custom-call(f32[128,128]{1,0:T(8,128)S(1)} %cholesky.621), custom_call_target="Cholesky" | custom-call | tf_op jit(solution)/shard_map/jit(cholesky)/cholesky | solution.py:122
  800.5 10.0 %custom-call.41 = f32[1,128,128]{1,2,0:T(8,128)S(1)} custom-call(f32[1,128,128]{2,1,0:T(8,128)S(1)} %get-tuple-element.65), custom_call_target="InvertDiagBlocksLowerTriangular" | custom-call | tf_op jit(solution)/shard_map/jit(cholesky)/cholesky | solution.py:122
  812.8 11.7 %cholesky.575 = f32[128,128]{1,0:T(8,128)S(1)} custom-call(f32[128,128]{1,0:T(8,128)S(1)} %convolution_subtract_fusion.15), custom_call_target="Cholesky" | custom-call | tf_op jit(solution)/shard_map/jit(cholesky)/cholesky | solution.py:122
  830.7 12.0 %while.8 = (s32[]{:T(128)}, f32[512,512]{1,0:T(8,128)}, s32[4,2]{0,1:T(2,128)S(1)}, f32[4,128,128]{2,1,0:T(8,128)S(1)}, s32[]{:T(128)}) while((s32[]{:T(128)}, f32[512,512]{1,0:T(8,128)}, s32[4,2]{0,1:T(2,128)S(1)}, f32[4,128,128]{2,1,0:T(8,128)S(1)}, s32[]{:T(128)}) %tuple.90), condition=%wide.while_cond.clone.1, body=%wide.while_body.clone.1.sunk | while | flops 2 | bytes 131181 | solution.py:27
  843.5 40.1 %custom-call.42 = f32[4,128,128]{1,2,0:T(8,128)S(1)} custom-call(f32[4,128,128]{2,1,0:T(8,128)} %copy-done.16), custom_call_target="InvertDiagBlocksLowerTriangular" | custom-call | tf_op jit(solution)/shard_map/jit(_solve_triangular)/triangular_solve | solution.py:27
  (263 shorter events, 221.2 us)
Async XLA Ops:
  7.2 82.9 %reduce-scatter.4.cloned.1.call-start = ((), (), s32[]{:S(2)}) async-start(), calls=%async_computation.2 | async-start | bytes 3342336
  28.1 112.1 %all-gather.2.cloned.1.call-start = ((), (), s32[]{:S(2)}) async-start(), calls=%async_computation.1 | async-start | bytes 6684672 | tf_op jit(solution)/shard_map/all_gather | solution.py:82
  92.2 196.1 %copy-start.3 = (f32[512,512]{1,0:T(8,128)}, f32[512,512]{1,0:T(8,128)S(1)}, u32[]{:S(2)}) copy-start(f32[512,512]{1,0:T(8,128)S(1)} %fusion.32) | copy-start | bytes 3145732
  148.7 1.0 copy-start.10
  288.9 7.7 slice-start
  289.4 7.3 slice-start.1
  302.1 8.1 copy-start.5
  302.9 6.3 collective-permute-start
  310.3 1.2 copy-start.7
  311.4 2.9 collective-permute-start.1
  315.7 0.8 copy-start.12
  316.5 7.7 collective-permute-start.2
  325.2 0.7 copy-start.11
  326.1 14.3 %collective-permute-start.3 = (f32[64,512]{0,1:T(8,128)S(1)}, f32[64,512]{0,1:T(8,128)}, u32[]{:S(2)}, u32[]{:S(2)}) collective-permute-start(f32[64,512]{0,1:T(8,128)S(1)} %constant_dynamic-slice_fusion.8), channel_id=1, source_target_pairs={{0,4},{1,5},{2,6},{3,7},{4,0},{5,1},{6,2},{7,3},{8,12},{9,13},{10,... | collective-permute-start | bytes 393224 | tf_op jit(solution)/shard_map/ppermute | solution.py:12
  342.3 17.4 %collective-permute-start.4 = (f32[32,512]{0,1:T(8,128)}, f32[32,512]{0,1:T(8,128)}, u32[]{:S(2)}, u32[]{:S(2)}) collective-permute-start(f32[32,512]{0,1:T(8,128)} %constant_dynamic-slice_fusion.7), channel_id=1, source_target_pairs={{0,8},{1,9},{2,10},{3,11},{4,12},{5,13},{6,14},{7,15},{8,0},{9,1},... | collective-permute-start | bytes 196616 | tf_op jit(solution)/shard_map/ppermute | solution.py:12
  361.7 7.6 collective-permute-start.5
  369.4 7.9 collective-permute-start.6
  378.4 14.8 %collective-permute-start.7 = (f32[2,64,512]{2,1,0:T(8,128)S(1)}, f32[2,64,512]{2,1,0:T(8,128)}, u32[]{:S(2)}, u32[]{:S(2)}) collective-permute-start(f32[2,64,512]{2,1,0:T(8,128)S(1)} %maximum_select_fusion.6), channel_id=1, source_target_pairs={{0,4},{1,5},{2,6},{3,7},{4,0},{5,1},{6,2},{7,3},{8,12},{9,13},{10,... | collective-permute-start | bytes 786440 | tf_op jit(solution)/shard_map/ppermute | solution.py:12
  395.1 13.3 %collective-permute-start.8 = (f32[2,128,512]{2,1,0:T(8,128)}, f32[2,128,512]{2,1,0:T(8,128)}, u32[]{:S(2)}, u32[]{:S(2)}) collective-permute-start(f32[2,128,512]{2,1,0:T(8,128)} %maximum_select_fusion.4), channel_id=1, source_target_pairs={{0,2},{1,3},{2,0},{3,1},{4,6},{5,7},{6,4},{7,5},{8,10},{9,11},{10,... | collective-permute-start | bytes 1572872 | tf_op jit(solution)/shard_map/ppermute | solution.py:12
  411.2 6.0 collective-permute-start.9
  412.6 190.8 %collective-permute-start.10 = (f32[512,512]{1,0:T(8,128)}, f32[512,512]{1,0:T(8,128)}, u32[]{:S(2)}, u32[]{:S(2)}) collective-permute-start(f32[512,512]{1,0:T(8,128)} %copy-done.5), channel_id=1, source_target_pairs={{0,16},{16,0},{32,48},{48,32},{64,80},{80,64},{96,112},{112,96},{1... | collective-permute-start | bytes 3145736 | tf_op jit(solution)/shard_map/ppermute | solution.py:12
  420.0 1.9 copy-start
  429.1 1.0 copy-start.8
  441.8 0.6 copy-start.15
  456.6 2.0 copy-start.13
  589.4 5.7 copy-start.14
  589.4 8.2 copy-start.1
  597.7 3.8 copy-start.6
  601.4 21.3 %copy-start.2 = (f32[512,512]{1,0:T(8,128)}, f32[512,512]{1,0:T(8,128)S(1)}, u32[]{:S(2)}) copy-start(f32[512,512]{1,0:T(8,128)S(1)} %fusion.33) | copy-start | bytes 3145732
  609.3 7.5 collective-permute-start.12
  614.2 7.5 collective-permute-start.11
  624.7 3.0 collective-permute-start.13
  627.9 7.6 collective-permute-start.14
  635.7 14.6 %collective-permute-start.15 = (f32[64,512]{0,1:T(8,128)S(1)}, f32[64,512]{0,1:T(8,128)S(1)}, u32[]{:S(2)}, u32[]{:S(2)}) collective-permute-start(f32[64,512]{0,1:T(8,128)S(1)} %constant_dynamic-slice_fusion.4), channel_id=1, source_target_pairs={{0,4},{1,5},{2,6},{3,7},{4,0},{5,1},{6,2},{7,3},{8,12},{9,13},{10,... | collective-permute-start | bytes 393224 | tf_op jit(solution)/shard_map/ppermute | solution.py:12
  650.5 16.4 %collective-permute-start.16 = (f32[32,512]{0,1:T(8,128)S(1)}, f32[32,512]{0,1:T(8,128)S(1)}, u32[]{:S(2)}, u32[]{:S(2)}) collective-permute-start(f32[32,512]{0,1:T(8,128)S(1)} %constant_dynamic-slice_fusion.3), channel_id=1, source_target_pairs={{0,8},{1,9},{2,10},{3,11},{4,12},{5,13},{6,14},{7,15},{8,0},{9,1},... | collective-permute-start | bytes 196616 | tf_op jit(solution)/shard_map/ppermute | solution.py:12
  667.1 7.5 collective-permute-start.17
  675.6 8.2 collective-permute-start.18
  684.9 7.8 collective-permute-start.19
  692.7 14.1 %collective-permute-start.20 = (f32[2,64,512]{2,1,0:T(8,128)S(1)}, f32[2,64,512]{2,1,0:T(8,128)S(1)}, u32[]{:S(2)}, u32[]{:S(2)}) collective-permute-start(f32[2,64,512]{2,1,0:T(8,128)S(1)} %maximum_select_fusion.7), channel_id=1, source_target_pairs={{0,4},{1,5},{2,6},{3,7},{4,0},{5,1},{6,2},{7,3},{8,12},{9,13},{10,... | collective-permute-start | bytes 786440 | tf_op jit(solution)/shard_map/ppermute | solution.py:12
  706.9 12.2 %collective-permute-start.21 = (f32[2,128,512]{2,1,0:T(8,128)S(1)}, f32[2,128,512]{2,1,0:T(8,128)S(1)}, u32[]{:S(2)}, u32[]{:S(2)}) collective-permute-start(f32[2,128,512]{2,1,0:T(8,128)S(1)} %maximum_select_fusion.5), channel_id=1, source_target_pairs={{0,2},{1,3},{2,0},{3,1},{4,6},{5,7},{6,4},{7,5},{8,10},{9,11},{10,... | collective-permute-start | bytes 1572872 | tf_op jit(solution)/shard_map/ppermute | solution.py:12
  720.2 4.9 collective-permute-start.22
  734.4 1.0 copy-start.9
  760.1 123.5 %copy-start.4 = (f32[512,512]{1,0:T(8,128)S(1)}, f32[512,512]{1,0:T(8,128)}, u32[]{:S(2)}) copy-start(f32[512,512]{1,0:T(8,128)} %copy-done.3) | copy-start | bytes 3145732
  842.8 0.7 copy-start.16
Sparse Core Ops, SparseCore 0:
  28.2 61.7 reduce-scatter.3
  92.2 47.9 all-gather.1
where the time goes:
time: 906 us; the launch traced here: 901 us
  other arithmetic  396 us (44%)
  waiting for transfers between devices  276 us (30%)
  matrix products  118 us (13%)
  local copies, waits for them, and re-layouts  60.8 us (7%)
  starting transfers between devices  26.4 us (3%)
  between operations  23.1 us (3%)
    ppermute x23, waiting for transfers between devices, swap(): lax.ppermute(block, axis, [(low, low ^ mask) for low in range(count)])  167 us
    another operation x7, other arithmetic, inverse_lower(): return jax.scipy.linalg.solve_triangular(factor, eye, lower=True)  127 us
    another operation x15, other arithmetic, on_device(): jnp.linalg.cholesky(transposed(parent_sample, parent_sample) + transposed...  83.9 us
    another operation x15, other arithmetic, on_device(): jnp.linalg.cholesky(transposed(grand_sample, grand_sample) + transposed(c...  81.2 us
    another operation x14, other arithmetic, on_device(): factor = jnp.linalg.cholesky(transposed(local, local))  79 us
    unnamed x3, waiting for transfers between devices  60.7 us
    dot_general x13, matrix products, transposed(): lax.dot_general(left, right, (((0,), (0,)), ((), ())), precision=HIGH, pr...  50.4 us
    all_gather x1, waiting for transfers between devices, on_device(): lax.all_gather(jnp.concatenate([sample_rows, owned], axis=1), 'tile', axi...  48 us
  transfers between devices with their start and end apart: 25, of which 23 were waited for; matrix products, arithmetic and copies ran while one was open for 22% of the time, Pallas kernels for 0%

commit v1 on v0

--- a/solution.py
+++ b/solution.py
@@ -5,6 +5,13 @@
 from jax.sharding import PartitionSpec as P
 
 HIGH = lax.Precision.HIGHEST
+
+
+def exchange_gather(value, axis, d):
+    n_dev = lax.axis_size(axis)
+    pieces = jnp.stack([value for _ in range(n_dev)])
+    pieces = lax.all_to_all(pieces, axis, split_axis=0, concat_axis=0)
+    return jnp.concatenate(pieces, axis=d)
 
 
 def swap(block, axis, mask):
@@ -79,7 +86,7 @@
     sample_rows = lax.psum_scatter(
         transposed(stacked, masked), "tile", scatter_dimension=0, tiled=True
     )
-    both = lax.all_gather(jnp.concatenate([sample_rows, owned], axis=1), "tile", axis=0, tiled=True)
+    both = exchange_gather(jnp.concatenate([sample_rows, owned], axis=1), "tile", 0)
     local = both[:, :rank_size]
     omega = both[:, rank_size:]
     factor = jnp.linalg.cholesky(transposed(local, local))

time: 906 us -> 1000 us (1.10)
  waiting for transfers between devices: 276 us -> 353 us
  starting transfers between devices: 26.4 us -> 42.5 us
    all_to_all x0 -> x1, waiting for transfers between devices: none -> 138 us  [exchange_gather(): pieces = lax.all_to_all(pieces, axis, split_axis=0, concat_axis=0)]
    all_gather x1 -> x0, waiting for transfers between devices: 48 us -> none  [on_device(): lax.all_gather(jnp.concatenate([sample_rows, owned], axis=1), 'tile', axi...]
    ppermute x23, waiting for transfers between devices: 167 us -> 154 us  [swap(): lax.ppermute(block, axis, [(low, low ^ mask) for low in range(count)])]
    unnamed x3 -> x2, waiting for transfers between devices: 60.7 us -> 60.9 us
  transfers between devices with their start and end apart: 25 -> 25, of which waited for: 23 -> 23; matrix products, arithmetic and copies ran while one was open for 22% -> 20% of each run, Pallas kernels for 0% -> 0%
where the time goes in v1:
time: 1000 us; the launch traced here: 997 us
  other arithmetic  396 us (40%)
  waiting for transfers between devices  353 us (35%)
  matrix products  120 us (12%)
  local copies, waits for them, and re-layouts  63 us (6%)
  starting transfers between devices  42.5 us (4%)
  between operations  22.9 us (2%)
    ppermute x23, waiting for transfers between devices, swap(): lax.ppermute(block, axis, [(low, low ^ mask) for low in range(count)])  154 us
    all_to_all x1, waiting for transfers between devices, exchange_gather(): pieces = lax.all_to_all(pieces, axis, split_axis=0, concat_axis=0)  138 us
    another operation x7, other arithmetic, inverse_lower(): return jax.scipy.linalg.solve_triangular(factor, eye, lower=True)  127 us
    another operation x15, other arithmetic, on_device(): jnp.linalg.cholesky(transposed(parent_sample, parent_sample) + transposed...  84.1 us
    another operation x15, other arithmetic, on_device(): jnp.linalg.cholesky(transposed(grand_sample, grand_sample) + transposed(c...  81.4 us
    another operation x14, other arithmetic, on_device(): factor = jnp.linalg.cholesky(transposed(local, local))  78.6 us
    unnamed x2, waiting for transfers between devices  60.9 us
    dot_general x13, matrix products, transposed(): lax.dot_general(left, right, (((0,), (0,)), ((), ())), precision=HIGH, pr...  52.2 us
  transfers between devices with their start and end apart: 25, of which 23 were waited for; matrix products, arithmetic and copies ran while one was open for 20% of the time, Pallas kernels for 0%

profile of v1, /device:TPU:1, one launch (start us, length us, event | category | flops | bytes accessed | tf_op | source)
XLA Modules:
  0.0 997.5 jit_solution(5022567667047509280)
XLA Ops:
  7.2 18.4 %convolution_bitcast_fusion = f32[1536,512]{0,1:T(8,128)S(1)} fusion(f32[16,96,1536]{2,1,0:T(8,128)} %param.5, f32[16,96,512]{2,1,0:T(8,128)} %param.6, pred[16]{0:T(512)(128)(4,1)S(1)} %iota_compare_fusion.4), kind=kOutput, calls=%fused_computation.6 | convolution fusion | flops 14496301056 | bytes 15728656 | tf_op jit(solution)/shard_map/dot_general | solution.py:27
  29.2 60.9 %reduce-scatter.4.cloned.1.call-done = f32[96,512]{1,0:T(8,128)} async-done(((f32[1536,512]{1,0:T(8,128)}), f32[96,512]{1,0:T(8,128)}) %reduce-scatter.4.cloned.1.call-update) | async-done | bytes 196624
  94.8 8.5 all-to-all-start
  103.4 138.0 %all-to-all-done = f32[16,96,1024]{2,1,0:T(8,128)} async-done(((f32[16,96,1024]{2,1,0:T(8,128)}), f32[16,96,1024]{2,1,0:T(8,128)}, u32[]{:S(2)}, u32[]{:S(2)}) %all-to-all-start) | async-done | bytes 6291488 | tf_op jit(solution)/shard_map/all_to_all | solution.py:13
  241.4 8.0 fusion.5
  251.0 11.7 %cholesky.374 = f32[128,128]{1,0:T(8,128)S(1)} custom-call(f32[128,128]{1,0:T(8,128)S(1)} %cholesky.586), custom_call_target="Cholesky" | custom-call | tf_op jit(solution)/shard_map/jit(cholesky)/cholesky | solution.py:92
  262.8 9.8 custom-call.31
  275.8 11.7 %cholesky.393 = f32[128,128]{1,0:T(8,128)S(1)} custom-call(f32[128,128]{1,0:T(8,128)S(1)} %cholesky.590), custom_call_target="Cholesky" | custom-call | tf_op jit(solution)/shard_map/jit(cholesky)/cholesky | solution.py:92
  287.6 9.8 custom-call.32
  298.9 11.7 %cholesky.414 = f32[128,128]{1,0:T(8,128)S(1)} custom-call(f32[128,128]{1,0:T(8,128)S(1)} %cholesky.595), custom_call_target="Cholesky" | custom-call | tf_op jit(solution)/shard_map/jit(cholesky)/cholesky | solution.py:92
  311.4 10.0 %custom-call.33 = f32[1,128,128]{1,2,0:T(8,128)S(1)} custom-call(f32[1,128,128]{2,1,0:T(8,128)S(1)} %get-tuple-element.85), custom_call_target="InvertDiagBlocksLowerTriangular" | custom-call | tf_op jit(solution)/shard_map/jit(cholesky)/cholesky | solution.py:92
  322.8 11.7 %cholesky.431 = f32[128,128]{1,0:T(8,128)S(1)} custom-call(f32[128,128]{1,0:T(8,128)S(1)} %convolution_subtract_fusion.17), custom_call_target="Cholesky" | custom-call | tf_op jit(solution)/shard_map/jit(cholesky)/cholesky | solution.py:92
  339.7 8.0 while.6
  347.7 39.7 %custom-call.34 = f32[4,128,128]{1,2,0:T(8,128)S(1)} custom-call(f32[4,128,128]{2,1,0:T(8,128)S(1)} %get-tuple-element.25), custom_call_target="InvertDiagBlocksLowerTriangular" | custom-call | tf_op jit(solution)/shard_map/jit(_solve_triangular)/triangular_solve | solution.py:34
  390.6 7.1 fusion.3
  397.7 7.2 fusion
  419.7 7.3 collective-permute-done.2
  431.4 11.6 %collective-permute-done.3 = f32[64,512]{0,1:T(8,128)} collective-permute-done((f32[64,512]{0,1:T(8,128)S(1)}, f32[64,512]{0,1:T(8,128)}, u32[]{:S(2)}, u32[]{:S(2)}) %collective-permute-start.3) | collective-permute-done | bytes 131104 | tf_op jit(solution)/shard_map/ppermute | solution.py:19
  448.5 14.2 %collective-permute-done.4 = f32[32,512]{0,1:T(8,128)} collective-permute-done((f32[32,512]{0,1:T(8,128)}, f32[32,512]{0,1:T(8,128)}, u32[]{:S(2)}, u32[]{:S(2)}) %collective-permute-start.4) | collective-permute-done | bytes 65568 | tf_op jit(solution)/shard_map/ppermute | solution.py:19
  466.6 5.1 collective-permute-done.5
  474.9 4.9 collective-permute-done.6
  480.9 12.1 %collective-permute-done.7 = f32[2,64,512]{2,1,0:T(8,128)} collective-permute-done((f32[2,64,512]{2,1,0:T(8,128)S(1)}, f32[2,64,512]{2,1,0:T(8,128)}, u32[]{:S(2)}, u32[]{:S(2)}) %collective-permute-start.7) | collective-permute-done | bytes 262176 | tf_op jit(solution)/shard_map/ppermute | solution.py:19
  494.9 12.2 %collective-permute-done.8 = f32[2,128,512]{2,1,0:T(8,128)} collective-permute-done((f32[2,128,512]{2,1,0:T(8,128)}, f32[2,128,512]{2,1,0:T(8,128)}, u32[]{:S(2)}, u32[]{:S(2)}) %collective-permute-start.8) | collective-permute-done | bytes 524320 | tf_op jit(solution)/shard_map/ppermute | solution.py:19
  529.4 11.7 %cholesky.446 = f32[128,128]{1,0:T(8,128)S(1)} custom-call(f32[128,128]{1,0:T(8,128)S(1)} %cholesky.599), custom_call_target="Cholesky" | custom-call | tf_op jit(solution)/shard_map/jit(cholesky)/cholesky | solution.py:112
  541.8 10.8 %custom-call.35 = f32[1,128,128]{1,2,0:T(8,128)} custom-call(f32[1,128,128]{2,1,0:T(8,128)S(1)} %get-tuple-element.81), custom_call_target="InvertDiagBlocksLowerTriangular" | custom-call | tf_op jit(solution)/shard_map/jit(cholesky)/cholesky | solution.py:112
  558.2 11.7 %cholesky.465 = f32[128,128]{1,0:T(8,128)S(1)} custom-call(f32[128,128]{1,0:T(8,128)S(1)} %cholesky.603), custom_call_target="Cholesky" | custom-call | tf_op jit(solution)/shard_map/jit(cholesky)/cholesky | solution.py:112
  573.5 9.8 custom-call.36
  586.6 12.3 %cholesky.486 = f32[128,128]{1,0:T(8,128)} custom-call(f32[128,128]{1,0:T(8,128)S(1)} %cholesky.608), custom_call_target="Cholesky" | custom-call | tf_op jit(solution)/shard_map/jit(cholesky)/cholesky | solution.py:112
  601.1 10.6 %custom-call.37 = f32[1,128,128]{1,2,0:T(8,128)} custom-call(f32[1,128,128]{2,1,0:T(8,128)S(1)} %get-tuple-element.75), custom_call_target="InvertDiagBlocksLowerTriangular" | custom-call | tf_op jit(solution)/shard_map/jit(cholesky)/cholesky | solution.py:112
  614.8 11.7 %cholesky.503 = f32[128,128]{1,0:T(8,128)S(1)} custom-call(f32[128,128]{1,0:T(8,128)S(1)} %convolution_subtract_fusion.16), custom_call_target="Cholesky" | custom-call | tf_op jit(solution)/shard_map/jit(cholesky)/cholesky | solution.py:112
  633.9 14.0 %while.7 = (s32[]{:T(128)}, f32[512,512]{1,0:T(8,128)}, s32[4,2]{0,1:T(2,128)S(1)}, f32[4,128,128]{2,1,0:T(8,128)}, s32[]{:T(128)}) while((s32[]{:T(128)}, f32[512,512]{1,0:T(8,128)}, s32[4,2]{0,1:T(2,128)S(1)}, f32[4,128,128]{2,1,0:T(8,128)}, s32[]{:T(128)}) %tuple.87), condition=%wide.while_cond.clone, body=%wide.while_body.clone.sunk | while | flops 2 | bytes 132705 | solution.py:34
  647.8 40.9 %custom-call.38 = f32[4,128,128]{1,2,0:T(8,128)} custom-call(f32[4,128,128]{2,1,0:T(8,128)} %get-tuple-element.26), custom_call_target="InvertDiagBlocksLowerTriangular" | custom-call | tf_op jit(solution)/shard_map/jit(_solve_triangular)/triangular_solve | solution.py:34
  727.8 7.5 collective-permute-done.14
  737.1 12.7 %collective-permute-done.15 = f32[64,512]{0,1:T(8,128)S(1)} collective-permute-done((f32[64,512]{0,1:T(8,128)S(1)}, f32[64,512]{0,1:T(8,128)S(1)}, u32[]{:S(2)}, u32[]{:S(2)}) %collective-permute-start.15) | collective-permute-done | bytes 131104 | tf_op jit(solution)/shard_map/ppermute | solution.py:19
  752.7 14.7 %collective-permute-done.16 = f32[32,512]{0,1:T(8,128)S(1)} collective-permute-done((f32[32,512]{0,1:T(8,128)S(1)}, f32[32,512]{0,1:T(8,128)S(1)}, u32[]{:S(2)}, u32[]{:S(2)}) %collective-permute-start.16) | collective-permute-done | bytes 65568 | tf_op jit(solution)/shard_map/ppermute | solution.py:19
  767.9 7.1 collective-permute-done.17
  778.1 6.1 collective-permute-done.18
  793.4 10.8 %collective-permute-done.20 = f32[2,64,512]{2,1,0:T(8,128)S(1)} collective-permute-done((f32[2,64,512]{2,1,0:T(8,128)S(1)}, f32[2,64,512]{2,1,0:T(8,128)S(1)}, u32[]{:S(2)}, u32[]{:S(2)}) %collective-permute-start.20) | collective-permute-done | bytes 262176 | tf_op jit(solution)/shard_map/ppermute | solution.py:19
  804.4 11.8 %collective-permute-done.21 = f32[2,128,512]{2,1,0:T(8,128)S(1)} collective-permute-done((f32[2,128,512]{2,1,0:T(8,128)S(1)}, f32[2,128,512]{2,1,0:T(8,128)S(1)}, u32[]{:S(2)}, u32[]{:S(2)}) %collective-permute-start.21) | collective-permute-done | bytes 524320 | tf_op jit(solution)/shard_map/ppermute | solution.py:19
  832.9 11.7 %cholesky.518 = f32[128,128]{1,0:T(8,128)S(1)} custom-call(f32[128,128]{1,0:T(8,128)S(1)} %cholesky.612), custom_call_target="Cholesky" | custom-call | tf_op jit(solution)/shard_map/jit(cholesky)/cholesky | solution.py:129
  845.7 9.8 custom-call.39
  858.8 12.1 %cholesky.537 = f32[128,128]{1,0:T(8,128)S(1)} custom-call(f32[128,128]{1,0:T(8,128)S(1)} %cholesky.616), custom_call_target="Cholesky" | custom-call | tf_op jit(solution)/shard_map/jit(cholesky)/cholesky | solution.py:129
  872.8 9.8 custom-call.40
  885.0 11.7 %cholesky.558 = f32[128,128]{1,0:T(8,128)S(1)} custom-call(f32[128,128]{1,0:T(8,128)S(1)} %cholesky.621), custom_call_target="Cholesky" | custom-call | tf_op jit(solution)/shard_map/jit(cholesky)/cholesky | solution.py:129
  898.0 9.9 custom-call.41
  910.2 11.7 %cholesky.575 = f32[128,128]{1,0:T(8,128)S(1)} custom-call(f32[128,128]{1,0:T(8,128)S(1)} %convolution_subtract_fusion.15), custom_call_target="Cholesky" | custom-call | tf_op jit(solution)/shard_map/jit(cholesky)/cholesky | solution.py:129
  928.2 11.5 %while.8 = (s32[]{:T(128)}, f32[512,512]{1,0:T(8,128)}, s32[4,2]{0,1:T(2,128)S(1)}, f32[4,128,128]{2,1,0:T(8,128)S(1)}, s32[]{:T(128)}) while((s32[]{:T(128)}, f32[512,512]{1,0:T(8,128)}, s32[4,2]{0,1:T(2,128)S(1)}, f32[4,128,128]{2,1,0:T(8,128)S(1)}, s32[]{:T(128)}) %tuple.88), condition=%wide.while_cond.clone.1, body=%wide.while_body.clone.1.sunk | while | flops 2 | bytes 131181 | solution.py:34
  940.4 40.1 %custom-call.42 = f32[4,128,128]{1,2,0:T(8,128)S(1)} custom-call(f32[4,128,128]{2,1,0:T(8,128)} %copy-done.16), custom_call_target="InvertDiagBlocksLowerTriangular" | custom-call | tf_op jit(solution)/shard_map/jit(_solve_triangular)/triangular_solve | solution.py:34
  (258 shorter events, 235.7 us)
Async XLA Ops:
  7.2 82.9 %reduce-scatter.4.cloned.1.call-start = ((), (), s32[]{:S(2)}) async-start(), calls=%async_computation.2 | async-start | bytes 3342336
  94.8 146.7 %all-to-all-start = ((f32[16,96,1024]{2,1,0:T(8,128)}), f32[16,96,1024]{2,1,0:T(8,128)}, u32[]{:S(2)}, u32[]{:S(2)}) async-start(f32[16,96,1024]{2,1,0:T(8,128)} %stack.14), calls=%async_computation | async-start | bytes 12582912 | tf_op jit(solution)/shard_map/all_to_all | solution.py:13
  103.4 286.1 %copy-start.3 = (f32[512,512]{1,0:T(8,128)}, f32[512,512]{1,0:T(8,128)S(1)}, u32[]{:S(2)}) copy-start(f32[512,512]{1,0:T(8,128)S(1)} %fusion.32) | copy-start | bytes 3145732
  250.0 1.0 copy-start.10
  404.9 7.4 copy-start.5
  405.7 5.6 collective-permute-start
  412.3 1.2 copy-start.7
  413.5 3.7 collective-permute-start.1
  418.5 0.8 copy-start.12
  419.3 7.7 collective-permute-start.2
  428.0 0.7 copy-start.11
  428.9 14.1 %collective-permute-start.3 = (f32[64,512]{0,1:T(8,128)S(1)}, f32[64,512]{0,1:T(8,128)}, u32[]{:S(2)}, u32[]{:S(2)}) collective-permute-start(f32[64,512]{0,1:T(8,128)S(1)} %constant_dynamic-slice_fusion.8), channel_id=1, source_target_pairs={{0,4},{1,5},{2,6},{3,7},{4,0},{5,1},{6,2},{7,3},{8,12},{9,13},{10,... | collective-permute-start | bytes 393224 | tf_op jit(solution)/shard_map/ppermute | solution.py:19
  444.9 17.7 %collective-permute-start.4 = (f32[32,512]{0,1:T(8,128)}, f32[32,512]{0,1:T(8,128)}, u32[]{:S(2)}, u32[]{:S(2)}) collective-permute-start(f32[32,512]{0,1:T(8,128)} %constant_dynamic-slice_fusion.7), channel_id=1, source_target_pairs={{0,8},{1,9},{2,10},{3,11},{4,12},{5,13},{6,14},{7,15},{8,0},{9,1},... | collective-permute-start | bytes 196616 | tf_op jit(solution)/shard_map/ppermute | solution.py:19
  464.6 7.2 collective-permute-start.5
  471.8 7.9 collective-permute-start.6
  480.8 12.2 %collective-permute-start.7 = (f32[2,64,512]{2,1,0:T(8,128)S(1)}, f32[2,64,512]{2,1,0:T(8,128)}, u32[]{:S(2)}, u32[]{:S(2)}) collective-permute-start(f32[2,64,512]{2,1,0:T(8,128)S(1)} %maximum_select_fusion.6), channel_id=1, source_target_pairs={{0,4},{1,5},{2,6},{3,7},{4,0},{5,1},{6,2},{7,3},{8,12},{9,13},{10,... | collective-permute-start | bytes 786440 | tf_op jit(solution)/shard_map/ppermute | solution.py:19
  494.9 12.2 %collective-permute-start.8 = (f32[2,128,512]{2,1,0:T(8,128)}, f32[2,128,512]{2,1,0:T(8,128)}, u32[]{:S(2)}, u32[]{:S(2)}) collective-permute-start(f32[2,128,512]{2,1,0:T(8,128)} %maximum_select_fusion.4), channel_id=1, source_target_pairs={{0,2},{1,3},{2,0},{3,1},{4,6},{5,7},{6,4},{7,5},{8,10},{9,11},{10,... | collective-permute-start | bytes 1572872 | tf_op jit(solution)/shard_map/ppermute | solution.py:19
  509.9 6.6 collective-permute-start.9
  512.3 190.4 %collective-permute-start.10 = (f32[512,512]{1,0:T(8,128)}, f32[512,512]{1,0:T(8,128)}, u32[]{:S(2)}, u32[]{:S(2)}) collective-permute-start(f32[512,512]{1,0:T(8,128)} %copy-done.5), channel_id=1, source_target_pairs={{0,16},{16,0},{32,48},{48,32},{64,80},{80,64},{96,112},{112,96},{1... | collective-permute-start | bytes 3145736 | tf_op jit(solution)/shard_map/ppermute | solution.py:19
  519.3 1.9 copy-start
  528.4 1.0 copy-start.8
  541.1 0.6 copy-start.15
  556.2 2.1 copy-start.13
  688.8 5.7 copy-start.14
  688.8 8.2 copy-start.1
  697.0 3.8 copy-start.6
  700.8 21.8 %copy-start.2 = (f32[512,512]{1,0:T(8,128)}, f32[512,512]{1,0:T(8,128)S(1)}, u32[]{:S(2)}) copy-start(f32[512,512]{1,0:T(8,128)S(1)} %fusion.33) | copy-start | bytes 3145732
  709.0 7.5 collective-permute-start.12
  714.0 7.5 collective-permute-start.11
  724.6 3.0 collective-permute-start.13
  727.7 7.6 collective-permute-start.14
  735.5 14.4 %collective-permute-start.15 = (f32[64,512]{0,1:T(8,128)S(1)}, f32[64,512]{0,1:T(8,128)S(1)}, u32[]{:S(2)}, u32[]{:S(2)}) collective-permute-start(f32[64,512]{0,1:T(8,128)S(1)} %constant_dynamic-slice_fusion.4), channel_id=1, source_target_pairs={{0,4},{1,5},{2,6},{3,7},{4,0},{5,1},{6,2},{7,3},{8,12},{9,13},{10,... | collective-permute-start | bytes 393224 | tf_op jit(solution)/shard_map/ppermute | solution.py:19
  750.1 17.2 %collective-permute-start.16 = (f32[32,512]{0,1:T(8,128)S(1)}, f32[32,512]{0,1:T(8,128)S(1)}, u32[]{:S(2)}, u32[]{:S(2)}) collective-permute-start(f32[32,512]{0,1:T(8,128)S(1)} %constant_dynamic-slice_fusion.3), channel_id=1, source_target_pairs={{0,8},{1,9},{2,10},{3,11},{4,12},{5,13},{6,14},{7,15},{8,0},{9,1},... | collective-permute-start | bytes 196616 | tf_op jit(solution)/shard_map/ppermute | solution.py:19
  767.5 7.5 collective-permute-start.17
  776.0 8.2 collective-permute-start.18
  785.3 7.8 collective-permute-start.19
  793.1 11.1 %collective-permute-start.20 = (f32[2,64,512]{2,1,0:T(8,128)S(1)}, f32[2,64,512]{2,1,0:T(8,128)S(1)}, u32[]{:S(2)}, u32[]{:S(2)}) collective-permute-start(f32[2,64,512]{2,1,0:T(8,128)S(1)} %maximum_select_fusion.7), channel_id=1, source_target_pairs={{0,4},{1,5},{2,6},{3,7},{4,0},{5,1},{6,2},{7,3},{8,12},{9,13},{10,... | collective-permute-start | bytes 786440 | tf_op jit(solution)/shard_map/ppermute | solution.py:19
  804.3 11.9 %collective-permute-start.21 = (f32[2,128,512]{2,1,0:T(8,128)S(1)}, f32[2,128,512]{2,1,0:T(8,128)S(1)}, u32[]{:S(2)}, u32[]{:S(2)}) collective-permute-start(f32[2,128,512]{2,1,0:T(8,128)S(1)} %maximum_select_fusion.5), channel_id=1, source_target_pairs={{0,2},{1,3},{2,0},{3,1},{4,6},{5,7},{6,4},{7,5},{8,10},{9,11},{10,... | collective-permute-start | bytes 1572872 | tf_op jit(solution)/shard_map/ppermute | solution.py:19
  817.3 5.1 collective-permute-start.22
  831.8 1.0 copy-start.9
  857.5 123.1 %copy-start.4 = (f32[512,512]{1,0:T(8,128)S(1)}, f32[512,512]{1,0:T(8,128)}, u32[]{:S(2)}) copy-start(f32[512,512]{1,0:T(8,128)} %copy-done.3) | copy-start | bytes 3145732
  939.7 0.7 copy-start.16
Sparse Core Ops, SparseCore 0:
  28.2 61.7 reduce-scatter.3
